TPU v7x, 256 devices: a whole 4x4x8 slice. The times are simulated.
256 devices in a mesh: dp: 32 (over y, z_hi, core), expert: 8 (over x, z_lo).
Axes of the slice: x: 4, y: 4, z: 8 (z_hi: 4, z_lo: 2; z = z_hi * 2 + z_lo), core: 2. Of those that a mesh axis runs over, the one named last changes fastest.
Arguments:
- tokens: bfloat16 [4096, 3072], P('dp', 'expert'), may hold values from -6 to 6
- out_grad: bfloat16 [4096, 3072], P('dp', 'expert'), may hold values from -6 to 6
- expert_ids: int32 [4096, 2], P('dp'), may hold values from 0 to 7, all different within a row; in each aligned block of 128 rows (0 to 127, 128 to 255, ...) at most 33 rows name the same one
- route_weights: float32 [4096, 2], P('dp'), may hold values from 0.2 to 1
- w_gate: bfloat16 [8, 3072, 8192], P('expert', None, 'dp'), may hold values from -0.109375 to 0.109375
- w_up: bfloat16 [8, 3072, 8192], P('expert', None, 'dp'), may hold values from -0.109375 to 0.109375
- w_down: bfloat16 [8, 8192, 3072], P('expert', 'dp'), may hold values from -0.0625 to 0.0625
Outputs:
- combined: bfloat16 [4096, 3072], P('dp', 'expert')
- d_gate: bfloat16 [8, 3072, 8192], P('expert', None, 'dp')
- d_up: bfloat16 [8, 3072, 8192], P('expert', None, 'dp')
- d_down: bfloat16 [8, 8192, 3072], P('expert', 'dp')
- d_route: float32 [4096, 2], P('dp')
Inputs may be any that keep to these rules, and one draw needn't show every extreme that they name: `expert_ids`: each token names 2 different experts; among the 128 tokens of one index of dp no expert is named more than 33 times, a bound that some block reaches.
All inputs are finite; a program needn't handle non-finite values.
Results may differ from a plain program's by a relative error of at most 0.02.
Values may be sent and summed in bfloat16 or wider, within the bound.
A program may use at most 128 MiB of HBM per device.

v0:
```python
import jax
import jax.numpy as jnp
from jax import lax
from jax.sharding import Mesh
from jax.sharding import PartitionSpec as P

highest = lax.Precision.HIGHEST
DP = ("dpo", "core")


def slot_table(routed, experts):
    flattened = routed.reshape(-1)
    onehot = (flattened[:, None] == jnp.arange(experts, dtype=jnp.int32)[None, :]).astype(jnp.int32)
    before = jnp.cumsum(onehot, axis=0) - onehot
    return jnp.sum(before * onehot, axis=1).reshape(routed.shape)


def pick_tables(routed, experts, capacity):
    places = slot_table(routed, experts)
    target = routed * capacity + places
    row_ids = jnp.arange(experts * capacity, dtype=jnp.int32)[:, None]
    return [
        (row_ids == target[None, :, which]).astype(jnp.float32) for which in range(routed.shape[1])
    ]


def local(tokens, out_grad, expert_ids, route_weights, w_gate, w_up, w_down):
    experts = lax.axis_size("expert")
    n_core = lax.axis_size("core")
    tok_rows, feat = tokens.shape
    top_count = expert_ids.shape[1]
    capacity = min(tok_rows, tok_rows * top_count * 33 // (32 * experts))
    picks = pick_tables(expert_ids, experts, capacity)
    dispatch = sum(picks)
    weighted = sum((picks[which] * route_weights[None, :, which] for which in range(top_count)))
    sent_tokens = jnp.dot(dispatch.astype(jnp.bfloat16), tokens, preferred_element_type=jnp.float32)
    sent_tokens = sent_tokens.astype(jnp.bfloat16).reshape(1, experts, capacity, feat)
    sent_grads = jnp.dot(weighted, out_grad.astype(jnp.float32), precision=highest)
    sent_grads = sent_grads.astype(jnp.bfloat16).reshape(1, experts, capacity, feat)
    sent_raw = jnp.dot(dispatch.astype(jnp.bfloat16), out_grad, preferred_element_type=jnp.float32)
    sent_raw = sent_raw.astype(jnp.bfloat16).reshape(1, experts, capacity, feat)
    sent = jnp.concatenate([sent_tokens, sent_grads, sent_raw], axis=0)
    recv = lax.all_to_all(sent, "expert", split_axis=1, concat_axis=3, tiled=True)
    both = jnp.concatenate([recv[0], recv[1]], axis=-1)
    blocks_all = lax.all_gather(both, DP, axis=0, tiled=True)
    n_blk = blocks_all.shape[0]
    d_all = recv.shape[-1]
    n_rows = n_blk * capacity
    flat_all = blocks_all.reshape(n_rows, 2 * d_all)
    gathered = flat_all[:, :d_all]
    grads_in = flat_all[:, d_all:]
    gate_slab = w_gate[0]
    up_slab = w_up[0]
    down_slab = w_down[0]
    gate_pre = jnp.dot(gathered, gate_slab, preferred_element_type=jnp.float32)
    up_pre = jnp.dot(gathered, up_slab, preferred_element_type=jnp.float32)
    sigmoid_gate = jax.nn.sigmoid(gate_pre)
    hidden = (gate_pre * sigmoid_gate * up_pre).astype(jnp.bfloat16)
    partial_out = jnp.dot(hidden, down_slab, preferred_element_type=jnp.float32).astype(
        jnp.bfloat16
    )
    d_hidden = jnp.einsum("rd,fd->rf", grads_in, down_slab, preferred_element_type=jnp.float32)
    d_down = jnp.einsum("rf,rd->fd", hidden, grads_in, preferred_element_type=jnp.float32).astype(
        jnp.bfloat16
    )
    d_gate_act = (
        d_hidden * up_pre * sigmoid_gate * (1.0 + gate_pre * (1.0 - sigmoid_gate))
    ).astype(jnp.bfloat16)
    d_up_act = (d_hidden * gate_pre * sigmoid_gate).astype(jnp.bfloat16)
    d_gate = jnp.einsum(
        "rd,rf->df", gathered, d_gate_act, preferred_element_type=jnp.float32
    ).astype(jnp.bfloat16)
    d_up = jnp.einsum("rd,rf->df", gathered, d_up_act, preferred_element_type=jnp.float32).astype(
        jnp.bfloat16
    )
    blocks = partial_out.reshape(n_blk, capacity, experts, d_all // experts).transpose(0, 2, 1, 3)
    summed_out = lax.psum_scatter(blocks, DP, scatter_dimension=0, tiled=True)
    raw_rows = recv[2, 0].reshape(capacity, experts, d_all // experts).astype(jnp.float32)
    dots = jnp.einsum("cfj,fcj->c", raw_rows, summed_out[0].astype(jnp.float32), precision=highest)
    hi = lax.reduce_precision(dots, exponent_bits=8, mantissa_bits=7)
    rest = dots - hi
    mid = lax.reduce_precision(rest, exponent_bits=8, mantissa_bits=7)
    lo = rest - mid
    pieces = jnp.stack([hi, mid, lo], axis=1).astype(jnp.bfloat16)
    lanes = jnp.pad(pieces, ((0, 0), (0, 128 - pieces.shape[1])))
    lanes = jnp.broadcast_to(lanes[None, None], (1, experts) + lanes.shape)
    payload = jnp.concatenate([summed_out, lanes], axis=-1)
    returned = lax.all_to_all(payload, "expert", split_axis=1, concat_axis=0, tiled=True)
    returned_out = returned[..., : d_all // experts]
    got = returned[..., d_all // experts : d_all // experts + 3].astype(jnp.float32)
    dots_all = (got[..., 0] + got[..., 1] + got[..., 2]).reshape(-1)
    flat_out = returned_out.reshape(experts * capacity, -1).astype(jnp.float32)
    combined = jnp.dot(weighted.T, flat_out, precision=highest).astype(jnp.bfloat16)
    target = expert_ids * capacity + slot_table(expert_ids, experts)
    d_route = dots_all[target]
    return (combined, d_gate[None], d_up[None], d_down[None], d_route)


def solution(mesh):
    n_dp, n_exp = mesh.devices.shape
    split = Mesh(mesh.devices.reshape(n_dp // 2, 2, n_exp), ("dpo", "core", "expert"))
    return jax.shard_map(
        local,
        mesh=split,
        in_specs=(
            P(DP, "expert"),
            P(DP, "expert"),
            P(DP, None),
            P(DP, None),
            P("expert", None, DP),
            P("expert", None, DP),
            P("expert", DP, None),
        ),
        out_specs=(
            P(DP, "expert"),
            P("expert", None, DP),
            P("expert", None, DP),
            P("expert", DP, None),
            P(DP, None),
        ),
        check_vma=False,
    )
```

profile of v0, /device:TPU:2, one launch (start us, length us, event | category | flops | bytes accessed | tf_op | source)
XLA Modules:
  0.0 306.3 jit_solution(1663517891706048601)
XLA Ops:
  7.2 0.0 copy-start
  7.2 0.0 all-gather.2.cloned.1.call-start
  7.2 0.9 copy.51
  8.1 0.1 eq.67
  8.3 0.1 eq.63
  8.4 0.6 reduce-window.6
  9.0 0.2 slice_reduce_fusion
  9.3 0.1 fusion.53
  9.4 0.1 reshape.80
  9.5 0.1 copy.53
  9.6 0.7 compare_select_fusion
  10.3 1.1 convolution_convert_fusion.1
  11.4 0.1 reshape.83
  11.5 0.8 slice_bitcast_fusion.3
  12.2 1.3 convolution_convert_fusion.2
  13.5 0.1 reshape.82
  13.6 0.0 copy-done.2
  13.6 0.2 convolution_convert_fusion.3
  13.8 0.1 reshape.81
  13.9 0.1 pad_maximum_fusion
  14.0 0.1 copy.54
  14.1 16.7 %all_to_all.27 = bf16[3,8,33,384]{3,2,0,1:T(8,128)(2,1)S(1)} all-to-all(bf16[3,8,33,384]{3,2,0,1:T(8,128)(2,1)S(1)} %copy.54), channel_id=1, replica_groups=mesh['dpo'=16,'core'=2,'expert'=8] {'expert'}, dimensions={1} | all-to-all | bytes 1216512 | tf_op jit(solution)/shard_map/all_to_all | solution.py:43
  30.8 0.1 fusion.63
  30.9 0.1 squeeze.22
  31.1 0.1 squeeze.21
  31.2 0.8 pad_maximum_fusion.1
  32.0 0.0 all-gather.2.cloned.1.call-update
  32.0 0.0 reduce-scatter.4.cloned.1.call-start
  32.1 106.2 %all-gather.2.cloned.1.call-done = bf16[32,33,6144]{2,1,0:T(8,128)(2,1)} async-done(((bf16[1,33,6144]{2,1,0:T(8,128)(2,1)}), bf16[32,33,6144]{2,1,0:T(8,128)(2,1)}) %all-gather.2.cloned.1.call-update) | async-done | bytes 12976144 | tf_op jit(solution)/shard_map/all_gather | solution.py:45
  138.3 11.8 %reshape.84 = bf16[1056,6144]{1,0:T(8,128)(2,1)} reshape(bf16[32,33,6144]{2,1,0:T(8,128)(2,1)} %all-gather.2.cloned.1.call-done) | data formatting | bytes 25952256 | tf_op jit(solution)/shard_map/reshape | solution.py:49
  150.1 5.3 %fusion.10 = f32[1056,256]{1,0:T(8,128)S(1)} fusion(bf16[1056,6144]{1,0:T(8,128)(2,1)} %reshape.84, bf16[1,3072,256]{2,1,0:T(8,128)(2,1)} %param.11), kind=kOutput, calls=%fused_computation.12 | convolution fusion | flops 1660944384 | bytes 9142272 | tf_op jit(solution)/shard_map/dot_general | solution.py:55
  155.4 1.7 copy-done.1
  157.1 0.4 copy-done.3
  157.5 2.9 multiply_convert_fusion.2
  160.4 0.0 copy-done.4
  160.4 1.9 convolution_convert_fusion
  162.3 4.4 %copy.67 = bf16[132,8,8,384]{3,2,1,0:T(8,128)(2,1)} copy(bf16[132,8,8,384]{3,1,2,0:T(8,128)(2,1)S(1)} %bitcast.71) | data formatting | bytes 12976128
  166.7 0.0 reduce-scatter.4.cloned.1.call-update
  166.7 0.1 copy.59
  166.8 0.1 reshape.89
  167.0 0.0 copy-start.5
  167.0 0.0 slice-start
  167.0 0.0 slice-start.1
  167.0 4.9 %fusion.2 = f32[1056,256]{1,0:T(8,128)S(1)} fusion(bf16[1056,6144]{1,0:T(8,128)(2,1)} %reshape.84, bf16[1,256,3072]{2,1,0:T(8,128)(2,1)S(1)} %copy-done), kind=kOutput, calls=%fused_computation.4 | convolution fusion | flops 1660944384 | bytes 9142272 | tf_op jit(solution)/shard_map/rd,fd->rf/dot_general | solution.py:62
  171.9 0.0 slice-start.2
  171.9 0.0 slice-start.3
  171.9 0.0 copy-start.6
  171.9 6.5 %fusion.24 = bf16[1,3072,256]{2,1,0:T(8,128)(2,1)} fusion(bf16[1056,6144]{1,0:T(8,128)(2,1)} %reshape.84, f32[1056,256]{1,0:T(8,128)S(1)} %fusion.2, f32[1056,256]{1,0:T(8,128)S(1)} %copy-done.5), kind=kOutput, calls=%fused_computation.18 | convolution fusion | flops 1663352832 | bytes 10223616 | tf_op jit(solution)/shard_map/rd,rf->df/dot_general | solution.py:73
  178.5 3.8 %fusion.27 = bf16[1,3072,256]{2,1,0:T(8,128)(2,1)} fusion(bf16[1056,6144]{1,0:T(8,128)(2,1)S(1)} %bitcast.74, f32[1056,256]{1,0:T(8,128)S(1)} %copy-done.5, f32[1056,256]{1,0:T(8,128)S(1)} %fusion.2, f32[1056,256]{1,0:T(8,128)S(1)} %copy-done.6), kind=kOutput, calls=%fused_computation.19 | convolution fusion | flops 1664434176 | bytes 11304960 | tf_op jit(solution)/shard_map/rd,rf->df/dot_general | solution.py:70
  182.3 98.7 %reduce-scatter.4.cloned.1.call-done = bf16[1,8,33,384]{3,1,2,0:T(8,128)(2,1)} async-done(((bf16[32,8,33,384]{3,1,2,0:T(8,128)(2,1)}), bf16[1,8,33,384]{3,1,2,0:T(8,128)(2,1)}) %reduce-scatter.4.cloned.1.call-update) | async-done | bytes 202768
  281.0 1.3 multiply_reduce_fusion
  282.3 0.1 copy.66
  282.4 1.0 pad_maximum_fusion.2
  283.4 0.8 copy.58
  284.2 4.8 %all-to-all-start.1 = ((bf16[1,8,33,512]{3,2,0,1:T(8,128)(2,1)}), bf16[1,8,33,512]{3,2,0,1:T(8,128)(2,1)S(1)}, u32[]{:S(2)}, u32[]{:S(2)}) async-start(bf16[1,8,33,512]{3,2,0,1:T(8,128)(2,1)} %copy.58), calls=%async_computation.1 | async-start | bytes 655360 | tf_op jit(solution)/shard_map/all_to_all | solution.py:88
  289.0 6.3 %fusion.21 = bf16[1,256,3072]{2,1,0:T(8,128)(2,1)} fusion(bf16[1056,256]{1,0:T(8,128)(2,1)S(1)} %get-tuple-element.42, bf16[1056,6144]{1,0:T(8,128)(2,1)} %reshape.84), kind=kOutput, calls=%fused_computation.17 | convolution fusion | flops 1661730816 | bytes 8601600 | tf_op jit(solution)/shard_map/rf,rd->fd/dot_general | solution.py:63
  295.3 0.0 all-to-all-done.1
  295.3 0.1 reshape.86
  295.4 1.1 convolution_convert_fusion.4
  296.5 0.2 fusion.37
  296.7 0.1 add.49
  296.8 2.0 gather_fusion
  298.7 0.1 reshape.88
  298.9 0.6 copy.60
  (25 shorter events, 0.2 us)
Async XLA Ops:
  7.2 153.3 %copy-start = (bf16[1,256,3072]{2,1,0:T(8,128)(2,1)S(1)}, bf16[1,256,3072]{2,1,0:T(8,128)(2,1)}, u32[]{:S(2)}) copy-start(bf16[1,256,3072]{2,1,0:T(8,128)(2,1)} %param.13) | copy-start | bytes 4718596
  7.2 6.4 %copy-start.2 = (bf16[128,384]{1,0:T(8,128)(2,1)S(1)}, bf16[128,384]{1,0:T(8,128)(2,1)}, u32[]{:S(2)}) copy-start(bf16[128,384]{1,0:T(8,128)(2,1)} %param.7) | copy-start | bytes 294916
  7.2 131.1 %all-gather.2.cloned.1.call-start = ((), (), s32[]{:S(2)}) async-start(), calls=%async_computation.3 | async-start | bytes 16220160 | tf_op jit(solution)/shard_map/all_gather | solution.py:45
  32.0 248.9 %reduce-scatter.4.cloned.1.call-start = ((), (), s32[]{:S(2)}) async-start(), calls=%async_computation.4 | async-start | bytes 6690816
  150.1 7.0 %copy-start.1 = (bf16[1056,6144]{1,0:T(8,128)(2,1)S(1)}, bf16[1056,6144]{1,0:T(8,128)(2,1)}, u32[]{:S(2)}) copy-start(bf16[1056,6144]{1,0:T(8,128)(2,1)} %reshape.84) | copy-start | bytes 38928388
  150.1 7.4 %copy-start.3 = (bf16[1,3072,256]{2,1,0:T(8,128)(2,1)S(1)}, bf16[1,3072,256]{2,1,0:T(8,128)(2,1)}, u32[]{:S(2)}) copy-start(bf16[1,3072,256]{2,1,0:T(8,128)(2,1)} %param.12) | copy-start | bytes 4718596
  157.5 2.9 copy-start.4
  167.0 4.9 %copy-start.5 = (f32[1056,256]{1,0:T(8,128)S(1)}, f32[1056,256]{1,0:T(8,128)}, u32[]{:S(2)}) copy-start(f32[1056,256]{1,0:T(8,128)} %copy-done.4) | copy-start | bytes 3244036
  167.0 11.5 %slice-start = ((s8[12976128]{0:T(1024)(128)(4,1)}), s8[4194304]{0:T(1024)(128)(4,1)S(1)}, s32[]{:S(2)}) async-start(s8[12976128]{0:T(1024)(128)(4,1)} %bitcast.73), calls=%async_computation.5 | async-start | bytes 8388608
  167.0 11.5 %slice-start.1 = ((s8[12976128]{0:T(1024)(128)(4,1)}), s8[4194304]{0:T(1024)(128)(4,1)S(1)}, s32[]{:S(2)}) async-start(s8[12976128]{0:T(1024)(128)(4,1)} %bitcast.73), calls=%async_computation.6 | async-start | bytes 8388608
  171.9 6.6 %slice-start.2 = ((s8[12976128]{0:T(1024)(128)(4,1)}), s8[4194304]{0:T(1024)(128)(4,1)S(1)}, s32[]{:S(2)}) async-start(s8[12976128]{0:T(1024)(128)(4,1)} %bitcast.73), calls=%async_computation.7 | async-start | bytes 8388608
  171.9 6.6 %slice-start.3 = ((s8[12976128]{0:T(1024)(128)(4,1)}), s8[393216]{0:T(1024)(128)(4,1)S(1)}, s32[]{:S(2)}) async-start(s8[12976128]{0:T(1024)(128)(4,1)} %bitcast.73), calls=%async_computation.8 | async-start | bytes 786432
  171.9 6.5 %copy-start.6 = (f32[1056,256]{1,0:T(8,128)S(1)}, f32[1056,256]{1,0:T(8,128)}, u32[]{:S(2)}) copy-start(f32[1056,256]{1,0:T(8,128)} %get-tuple-element.43) | copy-start | bytes 3244036
  284.2 11.1 %all-to-all-start.1 = ((bf16[1,8,33,512]{3,2,0,1:T(8,128)(2,1)}), bf16[1,8,33,512]{3,2,0,1:T(8,128)(2,1)S(1)}, u32[]{:S(2)}, u32[]{:S(2)}) async-start(bf16[1,8,33,512]{3,2,0,1:T(8,128)(2,1)} %copy.58), calls=%async_computation.1 | async-start | bytes 655360 | tf_op jit(solution)/shard_map/all_to_all | solution.py:88
Sparse Core Ops, SparseCore 0:
  32.2 106.0 all-gather.1
  166.8 114.1 reduce-scatter.3
where the time goes:
time: 307 us; the launch traced here: 306 us
  waiting for transfers between devices  205 us (67%)
  matrix products  35.2 us (11%)
  local copies, waits for them, and re-layouts  25.4 us (8%)
  blocking collectives  16.7 us (5%)
  between operations  14.4 us (5%)
  other arithmetic  4.92 us (2%)
  starting transfers between devices  4.86 us (2%)
    all_gather x1, waiting for transfers between devices, local(): blocks_all = lax.all_gather(both, DP, axis=0, tiled=True)  106 us
    unnamed x3, waiting for transfers between devices  98.7 us
    all_to_all x1, blocking collectives, local(): lax.all_to_all(sent, 'expert', split_axis=1, concat_axis=3, tiled=True)  16.7 us
    reshape x1, local copies, waits for them, and re-layouts, local(): flat_all = blocks_all.reshape(n_rows, 2 * d_all)  11.8 us
    unnamed x26, local copies, waits for them, and re-layouts  8.19 us
    dot_general x1, matrix products, local(): jnp.einsum('rd,rf->df', gathered, d_up_act, preferred_element_type=jnp.fl...  6.51 us
    dot_general x1, matrix products, local(): jnp.einsum('rf,rd->fd', hidden, grads_in, preferred_element_type=jnp.floa...  6.28 us
  transfers between devices with their start and end apart: 3, of which 2 were waited for; matrix products, arithmetic and copies ran while one was open for 7% of the time, Pallas kernels for 0%

commit v1 on v0

--- a/solution.py
+++ b/solution.py
@@ -42,7 +42,12 @@
     sent = jnp.concatenate([sent_tokens, sent_grads, sent_raw], axis=0)
     recv = lax.all_to_all(sent, "expert", split_axis=1, concat_axis=3, tiled=True)
     both = jnp.concatenate([recv[0], recv[1]], axis=-1)
-    blocks_all = lax.all_gather(both, DP, axis=0, tiled=True)
+
+    def islands_edit(local_block, row_dim):
+        part_next = lax.all_to_all(jnp.stack(lax.axis_size(DP) * [local_block], axis=0), DP, 0, 0)
+        return jnp.concatenate(part_next, axis=row_dim)
+
+    blocks_all = islands_edit(both, 0)
     n_blk = blocks_all.shape[0]
     d_all = recv.shape[-1]
     n_rows = n_blk * capacity

time: 307 us -> 545 us (1.78)
  blocking collectives: 16.7 us -> 355 us
  waiting for transfers between devices: 205 us -> 103 us
    all_to_all x0 -> x1, blocking collectives: none -> 339 us  [islands_edit(): lax.all_to_all(jnp.stack(lax.axis_size(DP) * [local_block], axis=0), DP,...]
    all_gather x1 -> x0, waiting for transfers between devices: 106 us -> none  [local(): blocks_all = lax.all_gather(both, DP, axis=0, tiled=True)]
    another operation x1 -> x3, local copies, waits for them, and re-layouts: 0.01 us -> 13.8 us  [the longest x1 11.8 us: local(): flat_all = blocks_all.reshape(n_rows, 2 * d_all)]
    reshape x1 -> x0, local copies, waits for them, and re-layouts: 11.8 us -> none  [local(): flat_all = blocks_all.reshape(n_rows, 2 * d_all)]
    unnamed x3 -> x2, waiting for transfers between devices: 98.7 us -> 103 us
  transfers between devices with their start and end apart: 3 -> 2, of which waited for: 2 -> 1; matrix products, arithmetic and copies ran while one was open for 7% -> 4% of each run, Pallas kernels for 0% -> 0%
where the time goes in v1:
time: 545 us
  blocking collectives  355 us (65%)
  waiting for transfers between devices  103 us (19%)
  matrix products  35.3 us (6%)
  local copies, waits for them, and re-layouts  27.4 us (5%)
  between operations  14.4 us (3%)
    all_to_all x1, blocking collectives, islands_edit(): lax.all_to_all(jnp.stack(lax.axis_size(DP) * [local_block], axis=0), DP,...  339 us
    unnamed x2, waiting for transfers between devices  103 us
    all_to_all x1, blocking collectives, local(): lax.all_to_all(sent, 'expert', split_axis=1, concat_axis=3, tiled=True)  16.7 us
    another operation x1, local copies, waits for them, and re-layouts, local(): flat_all = blocks_all.reshape(n_rows, 2 * d_all)  11.8 us
  transfers between devices with their start and end apart: 2, of which 1 were waited for; matrix products, arithmetic and copies ran while one was open for 4% of the time, Pallas kernels for 0%

profile of v1, /device:TPU:2, one launch (start us, length us, event | category | flops | bytes accessed | tf_op | source)
XLA Modules:
  0.0 544.7 jit_solution(12827543385427312132)
XLA Ops:
  7.2 0.0 copy-start
  7.2 0.0 reduce-scatter.4.cloned.1.call-start
  7.2 0.9 copy.51
  8.1 0.1 eq.67
  8.3 0.1 eq.63
  8.4 0.6 reduce-window.6
  9.0 0.2 slice_reduce_fusion
  9.3 0.1 fusion.53
  9.4 0.1 reshape.80
  9.5 0.1 copy.53
  9.6 0.7 compare_select_fusion
  10.3 1.1 convolution_convert_fusion.1
  11.4 0.1 reshape.83
  11.5 0.8 slice_bitcast_fusion.3
  12.2 1.3 convolution_convert_fusion.2
  13.5 0.1 reshape.82
  13.6 0.0 copy-done.3
  13.6 0.2 convolution_convert_fusion.3
  13.8 0.1 reshape.81
  13.9 0.1 pad_maximum_fusion
  14.0 0.1 copy.54
  14.1 16.7 %all_to_all.32 = bf16[3,8,33,384]{3,2,0,1:T(8,128)(2,1)S(1)} all-to-all(bf16[3,8,33,384]{3,2,0,1:T(8,128)(2,1)S(1)} %copy.54), channel_id=1, replica_groups=mesh['dpo'=16,'core'=2,'expert'=8] {'expert'}, dimensions={1} | all-to-all | bytes 1216512 | tf_op jit(solution)/shard_map/all_to_all | solution.py:43
  30.8 0.1 fusion.63
  30.9 0.1 squeeze.22
  31.1 0.1 squeeze.21
  31.2 2.0 stack.14
  33.3 338.8 %all_to_all.33 = bf16[32,1,33,6144]{3,2,1,0:T(8,128)(2,1)} all-to-all(bf16[32,1,33,6144]{3,2,1,0:T(8,128)(2,1)S(1)} %stack.14), channel_id=1, replica_groups=mesh['dpo'=16,'core'=2,'expert'=8] {'dpo','core'}, dimensions={0} | all-to-all | bytes 25952256 | tf_op jit(solution)/shard_map/all_to_all | solution.py:47
  372.1 11.8 %reshape_reshape.3 = bf16[1056,6144]{1,0:T(8,128)(2,1)} reshape(bf16[32,1,33,6144]{3,2,1,0:T(8,128)(2,1)} %all_to_all.33) | data formatting | bytes 25952256 | tf_op jit(solution)/shard_map/reshape;reshape | solution.py:54
  383.9 5.3 fusion.10
  389.2 1.7 copy-done.2
  390.9 0.4 copy-done.4
  391.3 2.9 multiply_convert_fusion.2
  394.2 1.9 convolution_convert_fusion
  396.0 4.4 copy.67
  400.4 0.0 reduce-scatter.4.cloned.1.call-update
  400.4 0.1 copy.59
  400.5 0.1 reshape.88
  400.7 0.0 copy-start.6
  400.7 0.0 slice-start
  400.7 0.0 slice-start.1
  400.7 4.9 fusion.2
  405.6 0.0 copy-done.6
  405.6 0.0 slice-start.2
  405.6 0.0 slice-start.3
  405.6 0.0 copy-start.7
  405.6 6.6 %fusion.24 = bf16[1,3072,256]{2,1,0:T(8,128)(2,1)} fusion(bf16[1056,6144]{1,0:T(8,128)(2,1)} %reshape_reshape.3, f32[1056,256]{1,0:T(8,128)S(1)} %fusion.2, f32[1056,256]{1,0:T(8,128)S(1)} %copy-done.6), kind=kOutput, calls=%fused_computation.18 | convolution fusion | flops 1663352832 | bytes 10223616 | tf_op jit(solution)/shard_map/rd,rf->df/dot_general | solution.py:78
  412.2 0.0 slice-done.3
  412.2 0.0 copy-done.7
  412.3 4.0 fusion.27
  416.3 103.0 %reduce-scatter.4.cloned.1.call-done = bf16[1,8,33,384]{3,1,2,0:T(8,128)(2,1)} async-done(((bf16[32,8,33,384]{3,1,2,0:T(8,128)(2,1)}), bf16[1,8,33,384]{3,1,2,0:T(8,128)(2,1)}) %reduce-scatter.4.cloned.1.call-update) | async-done | bytes 202768
  519.3 1.3 multiply_reduce_fusion
  520.6 0.1 copy.66
  520.7 1.0 pad_maximum_fusion.1
  521.7 0.8 copy.58
  522.5 4.8 all-to-all-start.2
  527.3 6.2 %fusion.21 = bf16[1,256,3072]{2,1,0:T(8,128)(2,1)} fusion(bf16[1056,256]{1,0:T(8,128)(2,1)S(1)} %get-tuple-element.42, bf16[1056,6144]{1,0:T(8,128)(2,1)} %reshape_reshape.3), kind=kOutput, calls=%fused_computation.17 | convolution fusion | flops 1661730816 | bytes 8601600 | tf_op jit(solution)/shard_map/rf,rd->fd/dot_general | solution.py:68
  533.6 0.0 all-to-all-done.2
  533.6 0.1 reshape.85
  533.7 1.1 convolution_convert_fusion.4
  534.8 0.2 fusion.37
  535.0 0.1 add.49
  535.1 2.0 gather_fusion
  537.0 0.1 reshape.87
  537.2 0.6 copy.60
  (26 shorter events, 0.3 us)
Async XLA Ops:
  7.2 387.0 %copy-start = (bf16[1,256,3072]{2,1,0:T(8,128)(2,1)S(1)}, bf16[1,256,3072]{2,1,0:T(8,128)(2,1)}, u32[]{:S(2)}) copy-start(bf16[1,256,3072]{2,1,0:T(8,128)(2,1)} %param.13) | copy-start | bytes 4718596
  7.2 6.4 %copy-start.3 = (bf16[128,384]{1,0:T(8,128)(2,1)S(1)}, bf16[128,384]{1,0:T(8,128)(2,1)}, u32[]{:S(2)}) copy-start(bf16[128,384]{1,0:T(8,128)(2,1)} %param.7) | copy-start | bytes 294916
  7.2 512.1 %reduce-scatter.4.cloned.1.call-start = ((), (), s32[]{:S(2)}) async-start(), calls=%async_computation.4 | async-start | bytes 6690816
  383.9 7.0 %copy-start.2 = (bf16[1056,6144]{1,0:T(8,128)(2,1)S(1)}, bf16[1056,6144]{1,0:T(8,128)(2,1)}, u32[]{:S(2)}) copy-start(bf16[1056,6144]{1,0:T(8,128)(2,1)} %reshape_reshape.3) | copy-start | bytes 38928388
  383.9 7.4 %copy-start.4 = (bf16[1,3072,256]{2,1,0:T(8,128)(2,1)S(1)}, bf16[1,3072,256]{2,1,0:T(8,128)(2,1)}, u32[]{:S(2)}) copy-start(bf16[1,3072,256]{2,1,0:T(8,128)(2,1)} %param.12) | copy-start | bytes 4718596
  391.3 2.9 copy-start.5
  400.7 4.9 copy-start.6
  400.7 11.5 %slice-start = ((s8[12976128]{0:T(1024)(128)(4,1)}), s8[4194304]{0:T(1024)(128)(4,1)S(1)}, s32[]{:S(2)}) async-start(s8[12976128]{0:T(1024)(128)(4,1)} %bitcast.75), calls=%async_computation.5 | async-start | bytes 8388608
  400.7 11.5 %slice-start.1 = ((s8[12976128]{0:T(1024)(128)(4,1)}), s8[4194304]{0:T(1024)(128)(4,1)S(1)}, s32[]{:S(2)}) async-start(s8[12976128]{0:T(1024)(128)(4,1)} %bitcast.75), calls=%async_computation.6 | async-start | bytes 8388608
  405.6 6.6 %slice-start.2 = ((s8[12976128]{0:T(1024)(128)(4,1)}), s8[4194304]{0:T(1024)(128)(4,1)S(1)}, s32[]{:S(2)}) async-start(s8[12976128]{0:T(1024)(128)(4,1)} %bitcast.75), calls=%async_computation.7 | async-start | bytes 8388608
  405.6 6.6 %slice-start.3 = ((s8[12976128]{0:T(1024)(128)(4,1)}), s8[393216]{0:T(1024)(128)(4,1)S(1)}, s32[]{:S(2)}) async-start(s8[12976128]{0:T(1024)(128)(4,1)} %bitcast.75), calls=%async_computation.8 | async-start | bytes 786432
  405.6 6.6 %copy-start.7 = (f32[1056,256]{1,0:T(8,128)S(1)}, f32[1056,256]{1,0:T(8,128)}, u32[]{:S(2)}) copy-start(f32[1056,256]{1,0:T(8,128)} %get-tuple-element.43) | copy-start | bytes 3244036
  522.5 11.1 %all-to-all-start.2 = ((bf16[1,8,33,512]{3,2,0,1:T(8,128)(2,1)}), bf16[1,8,33,512]{3,2,0,1:T(8,128)(2,1)S(1)}, u32[]{:S(2)}, u32[]{:S(2)}) async-start(bf16[1,8,33,512]{3,2,0,1:T(8,128)(2,1)} %copy.58), calls=%async_computation.2 | async-start | bytes 655360 | tf_op jit(solution)/shard_map/all_to_all | solution.py:93
  535.1 2.7 copy-start.1
Sparse Core Ops, SparseCore 0:
  400.5 118.6 reduce-scatter.3
